TPU v7x, 256 devices: a whole 4x4x8 slice. The times are simulated.
256 devices in a mesh: row: 8 (over y, core), col: 32 (over z, x).
Axes of the slice: x: 4, y: 4, z: 8, core: 2. Of those that a mesh axis runs over, the one named last changes fastest.
Arguments:
- solution: float32 [8, 32, 16, 128, 128], P('row', 'col'), may hold values from -6 to 6
- residual: float32 [8, 32, 16, 128, 128], P('row', 'col'), may hold values from -6 to 6, as said below
- prev_direction: float32 [8, 32, 16, 128, 128], P('row', 'col'), may hold values from -6 to 6, as said below
- prev_dot: float32 [128], replicated, may hold values from 262144 to 1048576
- face_lists: int32 [8, 32, 4, 4], P('row', 'col'), may hold values from 0 to 16, as said below
- multiplicity: int32 [8, 32, 16], P('row', 'col'), may hold values from 1 to 2, as said below
- block_pattern: int32 [8, 32, 16, 3], P('row', 'col'), may hold values from 0 to 15, as said below
- schur: float32 [8, 32, 16, 3, 128, 128], P('row', 'col'), may hold values from -1 to 4, as said below
- neumann_inverse: float32 [8, 32, 16, 3, 128, 128], P('row', 'col'), may hold values from 0 to 2, as said below
- coarse_basis: float32 [8, 32, 8, 2048], P('row', 'col'), may hold values from -0.25 to 0.25
- primal_map: int32 [8, 32, 8], P('row', 'col'), may hold values from 0 to 1023, all different within a row
- coarse_inverse: float32 [1024, 1024], P('col'), may hold values from -1 to 1, as said below
Outputs:
- new_solution: float32 [8, 32, 16, 128, 128], P('row', 'col')
- new_residual: float32 [8, 32, 16, 128, 128], P('row', 'col')
- direction: float32 [8, 32, 16, 128, 128], P('row', 'col')
Inputs may be any that keep to these rules, and one draw needn't show every extreme that they name: face_lists[i, j, f, k] names the interface blocks that subdomain (i, j) shares with its neighbour across face f (0 toward row i-1, 1 toward row i+1, 2 toward column j-1, 3 toward column j+1); slot k of a face names the same unknowns as slot k of the neighbour's list for the facing face, and both lists have the same length, 1 to 4 blocks, none on faces at the grid's edge; unused slots hold 16; no block lies on two faces; some face holds 4 blocks. multiplicity is 2 for blocks named in face_lists and 1 for the others. block_pattern[i, j, b, 0] = b; the two other entries of block row b are two other blocks, each of which lists b in turn. `schur`: each subdomain's Schur complement is symmetric positive definite, with positive diagonal and no positive entry off it. `neumann_inverse`: each subdomain's local solve matrix is symmetric positive definite. `coarse_inverse`: symmetric positive definite. `residual`: copies of an unknown held by two subdomains (slot k of facing lists) are equal. `prev_direction`: copies of an unknown held by two subdomains (slot k of facing lists) are equal.
All inputs are finite; a program needn't handle non-finite values.
Results may differ from a plain program's by a relative error of at most 0.0003.
Values sent between devices are 32-bit elements; how exact they have to be, the bound alone decides.
A program may use at most 128 MiB of HBM per device.

v0:
```python
import jax
import jax.numpy as jnp
from jax import lax
from jax.sharding import PartitionSpec as P

HIGH = lax.Precision.HIGHEST


def extended(cells, sides, width):
    for axis, dim in sides:
        count = lax.axis_size(axis)
        ends = count - 1
        head = lax.slice_in_dim(cells, 0, width, axis=dim)
        tail = lax.slice_in_dim(cells, cells.shape[dim] - width, cells.shape[dim], axis=dim)
        cells = jnp.concatenate(
            [
                lax.ppermute(tail, axis, [(i, (i + 1) % count) for i in range(ends)]),
                cells,
                lax.ppermute(head, axis, [((i + 1) % count, i) for i in range(ends)]),
            ],
            axis=dim,
        )
    return cells


def block_product(blocks, pattern, values_in):
    stacked_count, block_count, dofs, cases = values_in.shape
    gathered = jnp.take(values_in, pattern.reshape(-1), axis=1)
    gathered = gathered.reshape(stacked_count, block_count, pattern.shape[1], dofs, cases)
    return jnp.einsum("bkij,vbkjn->vbin", blocks, gathered, precision=HIGH)


def assemble(values_in, faces):
    stacked_count, block_count, dofs, cases = values_in.shape
    flattened = values_in.reshape(stacked_count, block_count, dofs * cases)
    indicator = (faces[..., None] == jnp.arange(block_count)).astype(jnp.float32)
    face_values = jnp.einsum("fkb,vbc->fvkc", indicator, flattened, precision=HIGH)
    row_faces = extended(face_values[0:2], (("row", 0),), 1)
    col_faces = extended(face_values[2:4], (("col", 0),), 1)
    received = jnp.stack([row_faces[0], row_faces[3], col_faces[0], col_faces[3]])
    added = jnp.einsum("fkb,fvkc->vbc", indicator, received, precision=HIGH)
    return (flattened + added).reshape(values_in.shape)


def precondition(residual, weight, faces, pattern, neumann, basis, primal_map, inverse_rows):
    scaled = residual * weight
    local_term = block_product(neumann, pattern, scaled[None])[0]
    cases = residual.shape[-1]
    coarse_local = jnp.dot(basis, scaled.reshape(-1, cases), precision=HIGH)
    owned_count, coarse_total_rows = inverse_rows.shape
    indicator = (primal_map[:, None] == jnp.arange(coarse_total_rows)).astype(jnp.float32)
    owned_rhs = lax.psum_scatter(
        jnp.dot(indicator.T, coarse_local, precision=HIGH), "col", scatter_dimension=0, tiled=True
    )
    owned_rhs = lax.psum(owned_rhs, "row")
    columns = inverse_rows
    owned_solution = jnp.dot(
        columns, lax.all_gather(owned_rhs, "col", axis=0, tiled=True), precision=HIGH
    )
    columns = indicator
    own_coarse = jnp.dot(
        columns, lax.all_gather(owned_solution, "col", axis=0, tiled=True), precision=HIGH
    )
    coarse_back = jnp.dot(basis.T, own_coarse, precision=HIGH).reshape(residual.shape)
    return assemble(((local_term + coarse_back) * weight)[None], faces)[0]


def per_device(
    solution,
    residual,
    prev_direction,
    prev_dot,
    face_lists,
    multiplicity,
    block_pattern,
    schur,
    neumann_inverse,
    coarse_basis,
    primal_map,
    coarse_inverse,
):
    faces = face_lists[0, 0]
    pattern = block_pattern[0, 0]
    weight = (1.0 / multiplicity[0, 0].astype(jnp.float32))[:, None, None]
    current = residual[0, 0]
    previous = prev_direction[0, 0]
    precond = precondition(
        current,
        weight,
        faces,
        pattern,
        neumann_inverse[0, 0],
        coarse_basis[0, 0],
        primal_map[0, 0],
        coarse_inverse,
    )
    local_precond_dot = jnp.sum(current * precond * weight, axis=(0, 1))
    precond_dot = lax.psum(local_precond_dot, ("row", "col"))
    direction_mix = precond_dot / prev_dot
    direction = precond + direction_mix * previous
    image = assemble(block_product(schur[0, 0], pattern, direction[None]), faces)[0]
    curvature = lax.psum(jnp.sum(direction * image * weight, axis=(0, 1)), ("row", "col"))
    step_size = precond_dot / curvature
    new_solution = solution[0, 0] + step_size * direction
    new_residual = current - step_size * image
    return (new_solution[None, None], new_residual[None, None], direction[None, None])


def solution(mesh):
    placed = (
        P("row", "col", None, None, None),
        P("row", "col", None, None, None),
        P("row", "col", None, None, None),
        P(),
        P("row", "col", None, None),
        P("row", "col", None),
        P("row", "col", None, None),
        P("row", "col", None, None, None, None),
        P("row", "col", None, None, None, None),
        P("row", "col", None, None),
        P("row", "col", None),
        P("col", None),
    )
    return jax.shard_map(
        per_device,
        mesh=mesh,
        in_specs=placed,
        out_specs=(
            P("row", "col", None, None, None),
            P("row", "col", None, None, None),
            P("row", "col", None, None, None),
        ),
        check_vma=False,
    )
```

profile of v0, /device:TPU:1, one launch (start us, length us, event | category | flops | bytes accessed | tf_op | source)
XLA Modules:
  0.0 597.9 jit_solution(11276702184320067996)
XLA Ops:
  7.2 0.0 copy-start
  7.2 0.0 reduce-scatter.2.cloned.1.call-start
  7.2 0.8 divide_bitcast_fusion
  8.0 1.5 broadcast_multiply_fusion
  9.5 1.5 fusion.35
  11.0 1.5 fusion.38
  12.5 0.0 reduce-scatter.2.cloned.1.call-update
  12.5 2.3 fusion.31
  14.9 0.1 copy.39
  14.9 0.1 reshape_squeeze.4
  15.1 3.6 gather_fusion
  18.7 2.2 bitcast_select_fusion.1
  20.9 0.0 copy-start.9
  20.9 6.2 %fusion.6 = f32[1,16,128,128]{2,3,1,0:T(8,128)} fusion(f32[16,3,128,128]{3,2,1,0:T(8,128)S(1)} %bitcast.147, f32[1,1,16,3,128,128]{5,4,3,2,1,0:T(8,128)S(1)} %copy-done), kind=kOutput, calls=%fused_computation.15 | convolution fusion | flops 1207959552 | bytes 7340032 | tf_op jit(solution)/shard_map/bkij,vbkjn->vbin/dot_general | solution.py:30
  27.1 2.6 copy.44
  29.7 194.6 %reduce-scatter.2.cloned.1.call-done = f32[32,128]{1,0:T(8,128)} async-done(((f32[1024,128]{1,0:T(8,128)}), f32[32,128]{1,0:T(8,128)}) %reduce-scatter.2.cloned.1.call-update) | async-done | bytes 16400 | tf_op jit(solution)/shard_map/reduce_scatter | solution.py:52
  224.3 26.4 %psum.21 = f32[32,128]{1,0:T(8,128)S(1)} all-reduce(f32[32,128]{1,0:T(8,128)} %reduce-scatter.2.cloned.1.call-done), channel_id=1, replica_groups=mesh['row'=8,'col'=32] {'row'}, use_global_device_ids=true, to_apply=%region_1.3 | all-reduce | flops 4096 | bytes 32768 | tf_op jit(solution)/shard_map/psum | solution.py:55
  250.7 35.9 %all_gather.6 = f32[1024,128]{1,0:T(8,128)S(1)} all-gather(f32[32,128]{1,0:T(8,128)S(1)} %psum.21), channel_id=1, replica_groups=mesh['row'=8,'col'=32] {'col'}, dimensions={0}, use_global_device_ids=true | all-gather | bytes 540672 | tf_op jit(solution)/shard_map/all_gather | solution.py:58
  286.5 0.4 convolution_bitcast_fusion.5
  286.9 0.0 copy-start.10
  287.0 35.8 %all_gather.7 = f32[1024,128]{1,0:T(8,128)S(1)} all-gather(f32[32,128]{1,0:T(8,128)S(1)} %convolution_bitcast_fusion.5), channel_id=1, replica_groups=mesh['row'=8,'col'=32] {'col'}, dimensions={0}, use_global_device_ids=true | all-gather | bytes 540672 | tf_op jit(solution)/shard_map/all_gather | solution.py:62
  322.7 0.3 fusion.37
  323.0 2.0 convolution_bitcast_fusion.4
  325.0 2.5 copy.42
  327.6 2.4 reshape.184
  329.9 3.0 convolution_bitcast_fusion.3
  333.0 0.9 fusion.48
  333.9 27.6 %collective-permute-start = (f32[1,1,4,16384]{3,2,0,1:T(4,128)}, f32[1,1,4,16384]{3,2,0,1:T(4,128)}, u32[]{:S(2)}, u32[]{:S(2)}) collective-permute-start(f32[1,1,4,16384]{3,2,0,1:T(4,128)} %get-tuple-element.10), channel_id=1, source_target_pairs={{0,32},{32,64},{64,96},{96,128},{128,160},{160,192},{192,224},{1,3... | collective-permute-start | bytes 786440 | tf_op jit(solution)/shard_map/ppermute | solution.py:17
  361.5 3.8 collective-permute-start.1
  365.4 3.1 collective-permute-start.2
  368.4 1.3 collective-permute-start.3
  369.7 2.5 copy.41
  372.2 2.4 squeeze.32
  374.6 2.4 reshape.183
  377.0 1.6 collective-permute-done.3
  378.6 3.4 fusion.1
  382.0 0.0 copy-start.4
  382.0 0.0 copy-start.13
  382.0 0.9 copy-done.4
  383.0 0.2 copy.54
  383.2 1.0 copy-done.2
  384.1 0.4 fusion.14
  384.5 78.4 %psum.22 = f32[128]{0:T(128)S(1)} all-reduce(f32[128]{0:T(128)S(1)} %fusion.14), channel_id=1, replica_groups=mesh['row'=8,'col'=32] {'row','col'}, use_global_device_ids=true, to_apply=%region_3.5 | all-reduce | flops 128 | bytes 1024 | tf_op jit(solution)/shard_map/psum | solution.py:98
  462.9 2.7 fusion.12
  465.5 3.6 gather_fusion.1
  469.1 2.3 bitcast_select_fusion
  471.5 0.5 copy-done.7
  472.0 6.3 %fusion.9 = f32[1,16,128,128]{2,3,1,0:T(8,128)} fusion(f32[16,3,128,128]{3,2,1,0:T(8,128)S(1)} %bitcast.146, f32[1,1,16,3,128,128]{5,4,3,2,1,0:T(8,128)S(1)} %copy-done.7), kind=kOutput, calls=%fused_computation.16 | convolution fusion | flops 1207959552 | bytes 7340032 | tf_op jit(solution)/shard_map/bkij,vbkjn->vbin/dot_general | solution.py:30
  478.3 2.5 copy.47
  480.8 2.4 reshape.224
  483.2 2.4 reshape.187
  485.6 2.4 convolution_bitcast_fusion.1
  488.0 0.1 fusion.47
  488.1 3.7 collective-permute-start.4
  491.8 1.9 collective-permute-start.5
  493.7 1.9 collective-permute-start.6
  495.7 1.3 collective-permute-start.7
  497.0 2.5 collective-permute-done.5
  499.5 2.2 collective-permute-done.6
  501.7 4.1 collective-permute-done.7
  505.8 1.2 multiply_reduce_fusion
  507.0 1.2 copy.57
  508.2 78.4 %psum.23 = f32[128]{0:T(128)S(1)} all-reduce(f32[128]{0:T(128)S(1)} %bitcast_reduce_fusion), channel_id=1, replica_groups=mesh['row'=8,'col'=32] {'row','col'}, use_global_device_ids=true, to_apply=%region_6.8 | all-reduce | flops 128 | bytes 1024 | tf_op jit(solution)/shard_map/psum | solution.py:102
  586.6 4.5 multiply_add_fusion
  (31 shorter events, 0.1 us)
Async XLA Ops:
  7.2 13.7 %copy-start = (f32[1,1,16,3,128,128]{5,4,3,2,1,0:T(8,128)S(1)}, f32[1,1,16,3,128,128]{5,4,3,2,1,0:T(8,128)}, u32[]{:S(2)}) copy-start(f32[1,1,16,3,128,128]{5,4,3,2,1,0:T(8,128)} %param.22) | copy-start | bytes 9437188
  7.2 3.8 copy-start.11
  7.2 217.1 %reduce-scatter.2.cloned.1.call-start = ((), (), s32[]{:S(2)}) async-start(), calls=%async_computation.1 | async-start | bytes 540672 | tf_op jit(solution)/shard_map/reduce_scatter | solution.py:52
  8.0 6.8 %copy-start.12 = (s32[1,1,16,3]{2,1,3,0:T(1,128)S(1)}, s32[1,1,16,3]{2,1,3,0:T(1,128)}, u32[]{:S(2)}) copy-start(s32[1,1,16,3]{2,1,3,0:T(1,128)} %param.20) | copy-start | bytes 580
  20.9 265.7 %copy-start.9 = (f32[32,1024]{1,0:T(8,128)S(1)}, f32[32,1024]{1,0:T(8,128)}, u32[]{:S(2)}) copy-start(f32[32,1024]{1,0:T(8,128)} %param.25) | copy-start | bytes 393220
  27.1 295.9 %copy-start.8 = (f32[1,1,8,2048]{3,2,1,0:T(8,128)S(1)}, f32[1,1,8,2048]{3,2,1,0:T(8,128)}, u32[]{:S(2)}) copy-start(f32[1,1,8,2048]{3,2,1,0:T(8,128)} %param.23) | copy-start | bytes 196612
  286.9 43.0 %copy-start.10 = (s32[1,1,4,4]{3,2,1,0:T(4,128)S(1)}, s32[1,1,4,4]{3,2,1,0:T(4,128)}, u32[]{:S(2)}) copy-start(s32[1,1,4,4]{3,2,1,0:T(4,128)} %param.18) | copy-start | bytes 196
  333.9 43.1 %collective-permute-start = (f32[1,1,4,16384]{3,2,0,1:T(4,128)}, f32[1,1,4,16384]{3,2,0,1:T(4,128)}, u32[]{:S(2)}, u32[]{:S(2)}) collective-permute-start(f32[1,1,4,16384]{3,2,0,1:T(4,128)} %get-tuple-element.10), channel_id=1, source_target_pairs={{0,32},{32,64},{64,96},{96,128},{128,160},{160,192},{192,224},{1,3... | collective-permute-start | bytes 786440 | tf_op jit(solution)/shard_map/ppermute | solution.py:17
  361.5 15.5 %collective-permute-start.1 = (f32[1,1,4,16384]{3,2,0,1:T(4,128)}, f32[1,1,4,16384]{3,2,0,1:T(4,128)}, u32[]{:S(2)}, u32[]{:S(2)}) collective-permute-start(f32[1,1,4,16384]{3,2,0,1:T(4,128)} %get-tuple-element.13), channel_id=1, source_target_pairs={{32,0},{64,32},{96,64},{128,96},{160,128},{192,160},{224,192},{33,... | collective-permute-start | bytes 786440 | tf_op jit(solution)/shard_map/ppermute | solution.py:19
  365.4 11.7 %collective-permute-start.2 = (f32[1,1,4,16384]{3,2,0,1:T(4,128)}, f32[1,1,4,16384]{3,2,0,1:T(4,128)}, u32[]{:S(2)}, u32[]{:S(2)}) collective-permute-start(f32[1,1,4,16384]{3,2,0,1:T(4,128)} %get-tuple-element.12), channel_id=1, source_target_pairs={{0,1},{1,2},{2,3},{3,4},{4,5},{5,6},{6,7},{7,8},{8,9},{9,10},{10,1... | collective-permute-start | bytes 786440 | tf_op jit(solution)/shard_map/ppermute | solution.py:17
  368.4 10.2 %collective-permute-start.3 = (f32[1,1,4,16384]{3,2,0,1:T(4,128)S(1)}, f32[1,1,4,16384]{3,2,0,1:T(4,128)}, u32[]{:S(2)}, u32[]{:S(2)}) collective-permute-start(f32[1,1,4,16384]{3,2,0,1:T(4,128)S(1)} %get-tuple-element.11), channel_id=1, source_target_pairs={{1,0},{2,1},{3,2},{4,3},{5,4},{6,5},{7,6},{8,7},{9,8},{10,9},{11,1... | collective-permute-start | bytes 786440 | tf_op jit(solution)/shard_map/ppermute | solution.py:19
  378.6 5.5 copy-start.1
  382.0 1.0 copy-start.4
  382.0 80.9 %copy-start.13 = (f32[128]{0:T(128)S(1)}, f32[128]{0:T(128)}, u32[]{:S(2)}) copy-start(f32[128]{0:T(128)} %param.17) | copy-start | bytes 1540
  383.2 1.0 copy-start.2
  469.1 2.8 copy-start.7
  485.6 20.1 %copy-start.3 = (f32[1,16,16384]{2,1,0:T(8,128)S(1)}, f32[1,16,16384]{2,1,0:T(8,128)}, u32[]{:S(2)}) copy-start(f32[1,16,16384]{2,1,0:T(8,128)} %squeeze.32) | copy-start | bytes 3145732
  485.6 20.1 %copy-start.5 = (f32[1,16,16384]{2,1,0:T(8,128)S(1)}, f32[1,16,16384]{2,1,0:T(8,128)}, u32[]{:S(2)}) copy-start(f32[1,16,16384]{2,1,0:T(8,128)} %copy-done.4) | copy-start | bytes 3145732
  485.6 20.1 %copy-start.6 = (f32[1,16,16384]{2,1,0:T(8,128)S(1)}, f32[1,16,16384]{2,1,0:T(8,128)}, u32[]{:S(2)}) copy-start(f32[1,16,16384]{2,1,0:T(8,128)} %reshape.187) | copy-start | bytes 3145732
  488.1 8.9 %collective-permute-start.4 = (f32[1,1,4,16384]{3,2,0,1:T(4,128)S(1)}, f32[1,1,4,16384]{3,2,0,1:T(4,128)S(1)}, u32[]{:S(2)}, u32[]{:S(2)}) collective-permute-start(f32[1,1,4,16384]{3,2,0,1:T(4,128)S(1)} %get-tuple-element.6), channel_id=1, source_target_pairs={{0,32},{32,64},{64,96},{96,128},{128,160},{160,192},{192,224},{1,3... | collective-permute-start | bytes 786440 | tf_op jit(solution)/shard_map/ppermute | solution.py:17
  491.8 7.7 %collective-permute-start.5 = (f32[1,1,4,16384]{3,2,0,1:T(4,128)S(1)}, f32[1,1,4,16384]{3,2,0,1:T(4,128)S(1)}, u32[]{:S(2)}, u32[]{:S(2)}) collective-permute-start(f32[1,1,4,16384]{3,2,0,1:T(4,128)S(1)} %get-tuple-element.9), channel_id=1, source_target_pairs={{32,0},{64,32},{96,64},{128,96},{160,128},{192,160},{224,192},{33,... | collective-permute-start | bytes 786440 | tf_op jit(solution)/shard_map/ppermute | solution.py:19
  493.7 7.9 %collective-permute-start.6 = (f32[1,1,4,16384]{3,2,0,1:T(4,128)S(1)}, f32[1,1,4,16384]{3,2,0,1:T(4,128)S(1)}, u32[]{:S(2)}, u32[]{:S(2)}) collective-permute-start(f32[1,1,4,16384]{3,2,0,1:T(4,128)S(1)} %get-tuple-element.8), channel_id=1, source_target_pairs={{0,1},{1,2},{2,3},{3,4},{4,5},{5,6},{6,7},{7,8},{8,9},{9,10},{10,1... | collective-permute-start | bytes 786440 | tf_op jit(solution)/shard_map/ppermute | solution.py:17
  495.7 10.1 %collective-permute-start.7 = (f32[1,1,4,16384]{3,2,0,1:T(4,128)S(1)}, f32[1,1,4,16384]{3,2,0,1:T(4,128)S(1)}, u32[]{:S(2)}, u32[]{:S(2)}) collective-permute-start(f32[1,1,4,16384]{3,2,0,1:T(4,128)S(1)} %get-tuple-element.7), channel_id=1, source_target_pairs={{1,0},{2,1},{3,2},{4,3},{5,4},{6,5},{7,6},{8,7},{9,8},{10,9},{11,1... | collective-permute-start | bytes 786440 | tf_op jit(solution)/shard_map/ppermute | solution.py:19
Sparse Core Ops, SparseCore 0:
  12.7 211.5 reduce-scatter.1
where the time goes:
time: 599 us; the launch traced here: 598 us
  blocking collectives  255 us (43%)
  waiting for transfers between devices  205 us (34%)
  starting transfers between devices  44.6 us (7%)
  local copies, waits for them, and re-layouts  34.4 us (6%)
  matrix products  28.1 us (5%)
  other arithmetic  16.6 us (3%)
  between operations  14.3 us (2%)
    reduce_scatter x1, waiting for transfers between devices, precondition(): lax.psum_scatter(jnp.dot(indicator.T, coarse_local, precision=HIGH), 'col...  195 us
    psum x1, blocking collectives, per_device(): lax.psum(jnp.sum(direction * image * weight, axis=(0, 1)), ('row', 'col'))  78.4 us
    psum x1, blocking collectives, per_device(): precond_dot = lax.psum(local_precond_dot, ('row', 'col'))  78.4 us
    ppermute x4, starting transfers between devices, extended(): lax.ppermute(tail, axis, [(i, (i + 1) % count) for i in range(ends)])  36.3 us
    all_gather x1, blocking collectives, precondition(): lax.all_gather(owned_rhs, 'col', axis=0, tiled=True)  35.9 us
    all_gather x1, blocking collectives, precondition(): lax.all_gather(owned_solution, 'col', axis=0, tiled=True)  35.8 us
    psum x1, blocking collectives, precondition(): owned_rhs = lax.psum(owned_rhs, 'row')  26.4 us
    dot_general x2, matrix products, block_product(): return jnp.einsum('bkij,vbkjn->vbin', blocks, gathered, precision=HIGH)  12.5 us
  transfers between devices with their start and end apart: 9, of which 5 were waited for; matrix products, arithmetic and copies ran while one was open for 4% of the time, Pallas kernels for 0%

commit v1 on v0

--- a/solution.py
+++ b/solution.py
@@ -59,7 +59,11 @@
     )
     columns = indicator
     own_coarse = jnp.dot(
-        columns, lax.all_gather(owned_solution, "col", axis=0, tiled=True), precision=HIGH
+        columns,
+        jnp.concatenate(
+            lax.all_to_all(jnp.stack([owned_solution] * lax.axis_size("col")), "col", 0, 0), axis=0
+        ),
+        precision=HIGH,
     )
     coarse_back = jnp.dot(basis.T, own_coarse, precision=HIGH).reshape(residual.shape)
     return assemble(((local_term + coarse_back) * weight)[None], faces)[0]

time: 599 us -> 574 us (0.958)
  blocking collectives: 255 us -> 218 us
  waiting for transfers between devices: 205 us -> 218 us
    all_gather x1 -> x0, blocking collectives: 35.8 us -> none  [precondition(): lax.all_gather(owned_solution, 'col', axis=0, tiled=True)]
    reduce_scatter x1, waiting for transfers between devices: 195 us -> 206 us  [precondition(): lax.psum_scatter(jnp.dot(indicator.T, coarse_local, precision=HIGH), 'col...]
    ppermute x4, starting transfers between devices: 36.3 us -> 26.1 us  [extended(): lax.ppermute(tail, axis, [(i, (i + 1) % count) for i in range(ends)])]
    all_to_all x0 -> x1, starting transfers between devices: none -> 7.09 us  [precondition(): lax.all_to_all(jnp.stack([owned_solution] * lax.axis_size('col')), 'col',...]
  transfers between devices with their start and end apart: 9 -> 10, of which waited for: 5 -> 6; matrix products, arithmetic and copies ran while one was open for 4% -> 4% of each run, Pallas kernels for 0% -> 0%
where the time goes in v1:
time: 574 us; the launch traced here: 573 us
  waiting for transfers between devices  218 us (38%)
  blocking collectives  218 us (38%)
  starting transfers between devices  42.5 us (7%)
  local copies, waits for them, and re-layouts  35.3 us (6%)
  matrix products  29.2 us (5%)
  other arithmetic  16.6 us (3%)
  between operations  14.3 us (2%)
    reduce_scatter x1, waiting for transfers between devices, precondition(): lax.psum_scatter(jnp.dot(indicator.T, coarse_local, precision=HIGH), 'col...  206 us
    psum x1, blocking collectives, per_device(): lax.psum(jnp.sum(direction * image * weight, axis=(0, 1)), ('row', 'col'))  78.4 us
    psum x1, blocking collectives, per_device(): precond_dot = lax.psum(local_precond_dot, ('row', 'col'))  76.9 us
    all_gather x1, blocking collectives, precondition(): lax.all_gather(owned_rhs, 'col', axis=0, tiled=True)  35.9 us
    psum x1, blocking collectives, precondition(): owned_rhs = lax.psum(owned_rhs, 'row')  26.4 us
    ppermute x4, starting transfers between devices, extended(): lax.ppermute(tail, axis, [(i, (i + 1) % count) for i in range(ends)])  26.1 us
    dot_general x2, matrix products, block_product(): return jnp.einsum('bkij,vbkjn->vbin', blocks, gathered, precision=HIGH)  12.5 us
  transfers between devices with their start and end apart: 10, of which 6 were waited for; matrix products, arithmetic and copies ran while one was open for 4% of the time, Pallas kernels for 0%

profile of v1, /device:TPU:1, one launch (start us, length us, event | category | flops | bytes accessed | tf_op | source)
XLA Modules:
  0.0 573.1 jit_solution(7170802521336095004)
XLA Ops:
  7.2 0.0 copy-start
  7.2 0.0 reduce-scatter.2.cloned.1.call-start
  7.2 0.8 divide_bitcast_fusion
  8.1 1.5 broadcast_multiply_fusion
  9.5 1.5 fusion.35
  11.0 1.5 fusion.38
  12.5 0.0 reduce-scatter.2.cloned.1.call-update
  12.5 0.1 copy.29
  12.6 0.1 reshape_squeeze.4
  12.7 2.3 fusion.31
  15.1 3.6 gather_fusion
  18.7 205.6 %reduce-scatter.2.cloned.1.call-done = f32[32,128]{1,0:T(8,128)} async-done(((f32[1024,128]{1,0:T(8,128)}), f32[32,128]{1,0:T(8,128)}) %reduce-scatter.2.cloned.1.call-update) | async-done | bytes 16400 | tf_op jit(solution)/shard_map/reduce_scatter | solution.py:52
  224.3 26.4 %psum.21 = f32[32,128]{1,0:T(8,128)S(1)} all-reduce(f32[32,128]{1,0:T(8,128)} %reduce-scatter.2.cloned.1.call-done), channel_id=1, replica_groups=mesh['row'=8,'col'=32] {'row'}, use_global_device_ids=true, to_apply=%region_1.3 | all-reduce | flops 4096 | bytes 32768 | tf_op jit(solution)/shard_map/psum | solution.py:55
  250.7 35.9 %all_gather.3 = f32[1024,128]{1,0:T(8,128)S(1)} all-gather(f32[32,128]{1,0:T(8,128)S(1)} %psum.21), channel_id=1, replica_groups=mesh['row'=8,'col'=32] {'col'}, dimensions={0}, use_global_device_ids=true | all-gather | bytes 540672 | tf_op jit(solution)/shard_map/all_gather | solution.py:58
  286.5 0.4 convolution_bitcast_fusion.5
  286.9 0.9 stack.6
  287.8 7.1 %all-to-all-start = ((f32[32,32,128]{2,1,0:T(8,128)}), f32[32,32,128]{2,1,0:T(8,128)}, u32[]{:S(2)}, u32[]{:S(2)}) async-start(f32[32,32,128]{2,1,0:T(8,128)} %stack.6), calls=%async_computation.1 | async-start | bytes 1048576 | tf_op jit(solution)/shard_map/all_to_all | solution.py:64
  294.9 2.2 bitcast_select_fusion.1
  297.1 0.0 copy-start.8
  297.1 6.2 %fusion.6 = f32[1,16,128,128]{2,3,1,0:T(8,128)} fusion(f32[16,3,128,128]{3,2,1,0:T(8,128)S(1)} %bitcast.148, f32[1,1,16,3,128,128]{5,4,3,2,1,0:T(8,128)S(1)} %copy-done), kind=kOutput, calls=%fused_computation.15 | convolution fusion | flops 1207959552 | bytes 7340032 | tf_op jit(solution)/shard_map/bkij,vbkjn->vbin/dot_general | solution.py:30
  303.3 2.5 copy.34
  305.9 1.7 all-to-all-done
  307.6 1.3 fusion.37
  308.9 2.0 convolution_bitcast_fusion.4
  310.9 2.5 copy.32
  313.5 2.4 reshape.190
  315.8 3.0 convolution_bitcast_fusion.3
  318.9 0.9 fusion.48
  319.8 17.5 %collective-permute-start = (f32[1,1,4,16384]{3,2,0,1:T(4,128)}, f32[1,1,4,16384]{3,2,0,1:T(4,128)}, u32[]{:S(2)}, u32[]{:S(2)}) collective-permute-start(f32[1,1,4,16384]{3,2,0,1:T(4,128)} %get-tuple-element.10), channel_id=1, source_target_pairs={{0,32},{32,64},{64,96},{96,128},{128,160},{160,192},{192,224},{1,3... | collective-permute-start | bytes 786440 | tf_op jit(solution)/shard_map/ppermute | solution.py:17
  337.4 4.8 collective-permute-start.1
  342.2 2.9 collective-permute-start.2
  345.2 1.3 collective-permute-start.3
  346.4 2.5 copy.31
  349.0 2.4 squeeze.32
  351.4 2.4 reshape.189
  353.8 1.6 collective-permute-done.3
  355.3 3.4 fusion.1
  358.7 0.9 copy-done.4
  359.7 0.2 copy.44
  359.9 0.0 copy-start.2
  359.9 1.0 copy-done.2
  360.9 0.4 fusion.14
  361.2 76.9 %psum.22 = f32[128]{0:T(128)S(1)} all-reduce(f32[128]{0:T(128)S(1)} %fusion.14), channel_id=1, replica_groups=mesh['row'=8,'col'=32] {'row','col'}, use_global_device_ids=true, to_apply=%region_3.5 | all-reduce | flops 128 | bytes 1024 | tf_op jit(solution)/shard_map/psum | solution.py:102
  438.1 2.7 fusion.12
  440.8 3.6 gather_fusion.1
  444.4 2.3 bitcast_select_fusion
  446.7 0.5 copy-done.7
  447.2 6.3 %fusion.9 = f32[1,16,128,128]{2,3,1,0:T(8,128)} fusion(f32[16,3,128,128]{3,2,1,0:T(8,128)S(1)} %bitcast.147, f32[1,1,16,3,128,128]{5,4,3,2,1,0:T(8,128)S(1)} %copy-done.7), kind=kOutput, calls=%fused_computation.16 | convolution fusion | flops 1207959552 | bytes 7340032 | tf_op jit(solution)/shard_map/bkij,vbkjn->vbin/dot_general | solution.py:30
  453.5 2.5 copy.37
  456.0 2.4 reshape.230
  458.4 2.4 reshape.193
  460.9 2.4 convolution_bitcast_fusion.1
  463.3 0.1 fusion.47
  463.4 3.7 collective-permute-start.4
  467.0 1.9 collective-permute-start.5
  469.0 1.9 collective-permute-start.6
  470.9 1.3 collective-permute-start.7
  472.2 2.5 collective-permute-done.5
  474.7 2.2 collective-permute-done.6
  476.9 4.1 collective-permute-done.7
  481.0 1.2 multiply_reduce_fusion
  482.2 1.2 copy.47
  483.4 78.4 %psum.23 = f32[128]{0:T(128)S(1)} all-reduce(f32[128]{0:T(128)S(1)} %bitcast_reduce_fusion), channel_id=1, replica_groups=mesh['row'=8,'col'=32] {'row','col'}, use_global_device_ids=true, to_apply=%region_6.8 | all-reduce | flops 128 | bytes 1024 | tf_op jit(solution)/shard_map/psum | solution.py:106
  561.8 4.5 multiply_add_fusion
  (33 shorter events, 0.1 us)
Async XLA Ops:
  7.2 289.9 %copy-start = (f32[1,1,16,3,128,128]{5,4,3,2,1,0:T(8,128)S(1)}, f32[1,1,16,3,128,128]{5,4,3,2,1,0:T(8,128)}, u32[]{:S(2)}) copy-start(f32[1,1,16,3,128,128]{5,4,3,2,1,0:T(8,128)} %param.22) | copy-start | bytes 9437188
  7.2 3.8 copy-start.11
  7.2 5.3 copy-start.12
  7.2 217.1 %reduce-scatter.2.cloned.1.call-start = ((), (), s32[]{:S(2)}) async-start(), calls=%async_computation.2 | async-start | bytes 540672 | tf_op jit(solution)/shard_map/reduce_scatter | solution.py:52
  15.1 271.4 %copy-start.9 = (f32[32,1024]{1,0:T(8,128)S(1)}, f32[32,1024]{1,0:T(8,128)}, u32[]{:S(2)}) copy-start(f32[32,1024]{1,0:T(8,128)} %param.25) | copy-start | bytes 393220
  287.8 19.8 %all-to-all-start = ((f32[32,32,128]{2,1,0:T(8,128)}), f32[32,32,128]{2,1,0:T(8,128)}, u32[]{:S(2)}, u32[]{:S(2)}) async-start(f32[32,32,128]{2,1,0:T(8,128)} %stack.6), calls=%async_computation.1 | async-start | bytes 1048576 | tf_op jit(solution)/shard_map/all_to_all | solution.py:64
  297.1 11.9 %copy-start.8 = (f32[1,1,8,2048]{3,2,1,0:T(8,128)S(1)}, f32[1,1,8,2048]{3,2,1,0:T(8,128)}, u32[]{:S(2)}) copy-start(f32[1,1,8,2048]{3,2,1,0:T(8,128)} %param.23) | copy-start | bytes 196612
  305.9 10.0 %copy-start.10 = (s32[1,1,4,4]{3,2,1,0:T(4,128)S(1)}, s32[1,1,4,4]{3,2,1,0:T(4,128)}, u32[]{:S(2)}) copy-start(s32[1,1,4,4]{3,2,1,0:T(4,128)} %param.18) | copy-start | bytes 196
  319.8 33.9 %collective-permute-start = (f32[1,1,4,16384]{3,2,0,1:T(4,128)}, f32[1,1,4,16384]{3,2,0,1:T(4,128)}, u32[]{:S(2)}, u32[]{:S(2)}) collective-permute-start(f32[1,1,4,16384]{3,2,0,1:T(4,128)} %get-tuple-element.10), channel_id=1, source_target_pairs={{0,32},{32,64},{64,96},{96,128},{128,160},{160,192},{192,224},{1,3... | collective-permute-start | bytes 786440 | tf_op jit(solution)/shard_map/ppermute | solution.py:17
  337.4 16.4 %collective-permute-start.1 = (f32[1,1,4,16384]{3,2,0,1:T(4,128)}, f32[1,1,4,16384]{3,2,0,1:T(4,128)}, u32[]{:S(2)}, u32[]{:S(2)}) collective-permute-start(f32[1,1,4,16384]{3,2,0,1:T(4,128)} %get-tuple-element.13), channel_id=1, source_target_pairs={{32,0},{64,32},{96,64},{128,96},{160,128},{192,160},{224,192},{33,... | collective-permute-start | bytes 786440 | tf_op jit(solution)/shard_map/ppermute | solution.py:19
  342.2 11.5 %collective-permute-start.2 = (f32[1,1,4,16384]{3,2,0,1:T(4,128)}, f32[1,1,4,16384]{3,2,0,1:T(4,128)}, u32[]{:S(2)}, u32[]{:S(2)}) collective-permute-start(f32[1,1,4,16384]{3,2,0,1:T(4,128)} %get-tuple-element.12), channel_id=1, source_target_pairs={{0,1},{1,2},{2,3},{3,4},{4,5},{5,6},{6,7},{7,8},{8,9},{9,10},{10,1... | collective-permute-start | bytes 786440 | tf_op jit(solution)/shard_map/ppermute | solution.py:17
  345.2 10.2 %collective-permute-start.3 = (f32[1,1,4,16384]{3,2,0,1:T(4,128)S(1)}, f32[1,1,4,16384]{3,2,0,1:T(4,128)}, u32[]{:S(2)}, u32[]{:S(2)}) collective-permute-start(f32[1,1,4,16384]{3,2,0,1:T(4,128)S(1)} %get-tuple-element.11), channel_id=1, source_target_pairs={{1,0},{2,1},{3,2},{4,3},{5,4},{6,5},{7,6},{8,7},{9,8},{10,9},{11,1... | collective-permute-start | bytes 786440 | tf_op jit(solution)/shard_map/ppermute | solution.py:19
  355.3 5.5 copy-start.1
  358.7 1.0 copy-start.4
  358.7 79.4 %copy-start.13 = (f32[128]{0:T(128)S(1)}, f32[128]{0:T(128)}, u32[]{:S(2)}) copy-start(f32[128]{0:T(128)} %param.17) | copy-start | bytes 1540
  359.9 1.0 copy-start.2
  444.4 2.8 copy-start.7
  460.9 20.1 %copy-start.3 = (f32[1,16,16384]{2,1,0:T(8,128)S(1)}, f32[1,16,16384]{2,1,0:T(8,128)}, u32[]{:S(2)}) copy-start(f32[1,16,16384]{2,1,0:T(8,128)} %squeeze.32) | copy-start | bytes 3145732
  460.9 20.1 %copy-start.5 = (f32[1,16,16384]{2,1,0:T(8,128)S(1)}, f32[1,16,16384]{2,1,0:T(8,128)}, u32[]{:S(2)}) copy-start(f32[1,16,16384]{2,1,0:T(8,128)} %copy-done.4) | copy-start | bytes 3145732
  460.9 20.1 %copy-start.6 = (f32[1,16,16384]{2,1,0:T(8,128)S(1)}, f32[1,16,16384]{2,1,0:T(8,128)}, u32[]{:S(2)}) copy-start(f32[1,16,16384]{2,1,0:T(8,128)} %reshape.193) | copy-start | bytes 3145732
  463.4 8.8 %collective-permute-start.4 = (f32[1,1,4,16384]{3,2,0,1:T(4,128)S(1)}, f32[1,1,4,16384]{3,2,0,1:T(4,128)S(1)}, u32[]{:S(2)}, u32[]{:S(2)}) collective-permute-start(f32[1,1,4,16384]{3,2,0,1:T(4,128)S(1)} %get-tuple-element.6), channel_id=1, source_target_pairs={{0,32},{32,64},{64,96},{96,128},{128,160},{160,192},{192,224},{1,3... | collective-permute-start | bytes 786440 | tf_op jit(solution)/shard_map/ppermute | solution.py:17
  467.0 7.7 %collective-permute-start.5 = (f32[1,1,4,16384]{3,2,0,1:T(4,128)S(1)}, f32[1,1,4,16384]{3,2,0,1:T(4,128)S(1)}, u32[]{:S(2)}, u32[]{:S(2)}) collective-permute-start(f32[1,1,4,16384]{3,2,0,1:T(4,128)S(1)} %get-tuple-element.9), channel_id=1, source_target_pairs={{32,0},{64,32},{96,64},{128,96},{160,128},{192,160},{224,192},{33,... | collective-permute-start | bytes 786440 | tf_op jit(solution)/shard_map/ppermute | solution.py:19
  469.0 7.9 %collective-permute-start.6 = (f32[1,1,4,16384]{3,2,0,1:T(4,128)S(1)}, f32[1,1,4,16384]{3,2,0,1:T(4,128)S(1)}, u32[]{:S(2)}, u32[]{:S(2)}) collective-permute-start(f32[1,1,4,16384]{3,2,0,1:T(4,128)S(1)} %get-tuple-element.8), channel_id=1, source_target_pairs={{0,1},{1,2},{2,3},{3,4},{4,5},{5,6},{6,7},{7,8},{8,9},{9,10},{10,1... | collective-permute-start | bytes 786440 | tf_op jit(solution)/shard_map/ppermute | solution.py:17
  470.9 10.1 %collective-permute-start.7 = (f32[1,1,4,16384]{3,2,0,1:T(4,128)S(1)}, f32[1,1,4,16384]{3,2,0,1:T(4,128)S(1)}, u32[]{:S(2)}, u32[]{:S(2)}) collective-permute-start(f32[1,1,4,16384]{3,2,0,1:T(4,128)S(1)} %get-tuple-element.7), channel_id=1, source_target_pairs={{1,0},{2,1},{3,2},{4,3},{5,4},{6,5},{7,6},{8,7},{9,8},{10,9},{11,1... | collective-permute-start | bytes 786440 | tf_op jit(solution)/shard_map/ppermute | solution.py:19
Sparse Core Ops, SparseCore 0:
  12.7 211.5 reduce-scatter.1
